TPU v7x, 32 devices: a whole 2x2x4 slice. The times are simulated.
32 devices in a mesh: lat: 4 (over z), lon: 8 (over y, x, core).
Axes of the slice: x: 2, y: 2, z: 4, core: 2. Of those that a mesh axis runs over, the one named last changes fastest.
Arguments:
- layer_input: float32 [4, 768, 90, 180], P('lat', 'lon'), may hold values from -6 to 6
- grad_output: float32 [4, 768, 90, 180], P('lat', 'lon'), may hold values from -6 to 6
- first_weight: float32 [2, 8, 96, 96], replicated, may hold values from -0.625 to 0.625
- first_bias: float32 [2, 8, 96], replicated, may hold values from -3 to 3
- second_weight: float32 [2, 8, 96, 96], replicated, may hold values from -0.625 to 0.625
- second_bias: float32 [2, 8, 96], replicated, may hold values from -3 to 3
Outputs:
- grad_input: float32 [4, 768, 90, 180], P('lat', 'lon')
- grad_first_weight: float32 [2, 8, 96, 96], replicated
- grad_first_bias: float32 [2, 8, 96], replicated
- grad_second_weight: float32 [2, 8, 96, 96], replicated
- grad_second_bias: float32 [2, 8, 96], replicated
All inputs are finite; a program needn't handle non-finite values.
Results may differ from a plain program's by a relative error of at most 0.0003.
Values sent between devices are 32-bit elements; how exact they have to be, the bound alone decides.
No kernel may reach another device: no remote copies, remote signals or barrier semaphores. Data moves between devices by JAX's collectives and lax.ppermute only.
A program may use at most 192 MiB of HBM per device.

v0:
```python
import math
import jax
import jax.numpy as jnp
from jax import lax
from jax.sharding import PartitionSpec as P

SHRINK = 0.01
GELU_SCALE = math.sqrt(2.0 / math.pi)
GELU_CUBE = 0.044715
HIGHEST = lax.Precision.HIGHEST


def tables(length, count, limit):
    first = jnp.arange(length, dtype=jnp.int32)[:, None]
    second = jnp.arange(count, dtype=jnp.int32)[None, :]
    angle = 2.0 * math.pi / length * (first * second % length).astype(jnp.float32)
    keeper = (second < limit).astype(jnp.float32) / math.sqrt(length)
    return (jnp.cos(angle) * keeper, jnp.sin(angle) * keeper)


def cotangent_weight(length, count):
    index = jnp.arange(count, dtype=jnp.int32)
    edge = (index == 0) | (2 * index == length)
    return jnp.where(edge, 1.0, 2.0).astype(jnp.float32)


def gelu_slope(value):
    inner = GELU_SCALE * (value + GELU_CUBE * value * value * value)
    tangent = jnp.tanh(inner)
    return 0.5 * (1.0 + tangent) + 0.5 * value * (1.0 - tangent * tangent) * GELU_SCALE * (
        1.0 + 3.0 * GELU_CUBE * value * value
    )


def complex_matrix(weight):
    real_part = weight[0]
    imag_part = weight[1]
    upper = jnp.stack([real_part, imag_part], axis=2)
    lower = jnp.stack([-imag_part, real_part], axis=2)
    return jnp.stack([upper, lower], axis=1)


def forward_mix(left, matrix):
    return jnp.einsum("psbir,bpiqj->qsbjr", left, matrix, precision=HIGHEST)


def back_mix(left, matrix):
    return jnp.einsum("qsbjr,bpiqj->psbir", left, matrix, precision=HIGHEST)


def weight_grad(left, right):
    total = jnp.einsum("psbir,qsbjr->bpiqj", left, right, precision=HIGHEST)
    grad_real = total[:, 0, :, 0, :] + total[:, 1, :, 1, :]
    grad_imag = total[:, 0, :, 1, :] - total[:, 1, :, 0, :]
    return jnp.stack([grad_real, grad_imag])


def bias_view(vector):
    return vector[:, None, :, :, None]


def block_backward(x_both, g_both, first_weight, first_bias, second_weight, second_bias):
    parts, samples, channels, modes = x_both.shape
    blocks = first_weight.shape[1]
    width = first_weight.shape[2]
    shape_five = (parts, samples, blocks, width, modes)
    x_both = x_both.reshape(shape_five)
    g_both = g_both.reshape(shape_five)
    first_matrix = complex_matrix(first_weight)
    second_matrix = complex_matrix(second_weight)
    a_both = forward_mix(x_both, first_matrix) + bias_view(first_bias)
    o_both = jax.nn.gelu(a_both, approximate=True)
    z_both = forward_mix(o_both, second_matrix) + bias_view(second_bias)
    e_both = g_both * jnp.tanh(z_both / SHRINK) ** 2
    grad_w_two = weight_grad(o_both, e_both)
    grad_b_two = jnp.sum(e_both, axis=(1, 4))
    s_both = back_mix(e_both, second_matrix) * gelu_slope(a_both)
    grad_w_one = weight_grad(x_both, s_both)
    grad_b_one = jnp.sum(s_both, axis=(1, 4))
    d_both = back_mix(s_both, first_matrix)
    return (
        d_both.reshape((parts, samples, channels, modes)),
        (grad_w_one, grad_b_one, grad_w_two, grad_b_two),
    )


def on_device(layer_input, grad_output, first_weight, first_bias, second_weight, second_bias):
    lon_count = lax.axis_size("lon")
    samples, local_ch, lat_rows, lon_cols = layer_input.shape
    kept_freqs = lon_cols // 2 + 1
    freq_slots = (lon_cols // 2 + lon_count) // lon_count * lon_count
    lon_cos, lon_sin = tables(lon_cols, freq_slots, kept_freqs)
    factor_row = cotangent_weight(lon_cols, freq_slots)[None, :]
    lon_table = jnp.stack([lon_cos, -lon_sin], axis=1)
    cot_table = jnp.stack([lon_cos * factor_row, -lon_sin * factor_row], axis=1)
    lon_back = jnp.stack([lon_cos.T, -lon_sin.T])
    lat_cos, lat_sin = tables(lat_rows, lat_rows, lat_rows)
    lat_table = jnp.stack(
        [jnp.stack([lat_cos, -lat_sin], axis=1), jnp.stack([lat_sin, lat_cos], axis=1)]
    )
    lat_back = jnp.stack(
        [jnp.stack([lat_cos, lat_sin], axis=1), jnp.stack([-lat_sin, lat_cos], axis=1)]
    )

    def lon_forward(data, table):
        return jnp.einsum("schw,wqk->qsckh", data, table, precision=HIGHEST)

    def lat_forward(data):
        return jnp.einsum("psckh,phqm->qsckm", data, lat_table, precision=HIGHEST)

    x_both = lon_forward(layer_input, lon_table)
    g_both = lon_forward(grad_output, cot_table)
    x_both = lat_forward(x_both)
    g_both = lat_forward(g_both)
    flat_shape = (2, samples, local_ch, freq_slots * lat_rows)
    x_modes, g_modes = (
        lax.all_to_all(x_both.reshape(flat_shape), "lon", split_axis=3, concat_axis=2, tiled=True),
        lax.all_to_all(g_both.reshape(flat_shape), "lon", split_axis=3, concat_axis=2, tiled=True),
    )
    d_stack, partial_grads = block_backward(
        x_modes, g_modes, first_weight, first_bias, second_weight, second_bias
    )
    stacked = lax.all_to_all(d_stack, "lon", split_axis=2, concat_axis=3, tiled=True)
    shape_five = (2, stacked.shape[1], stacked.shape[2], freq_slots, lat_rows)
    grad_input = jnp.einsum(
        "qsckh,qkw->schw",
        jnp.einsum("psckm,pmqh->qsckh", stacked.reshape(shape_five), lat_back, precision=HIGHEST),
        lon_back,
        precision=HIGHEST,
    )
    flat_grads = jnp.concatenate([piece.reshape(-1) for piece in partial_grads])
    share = lax.psum_scatter(flat_grads, "lon", scatter_dimension=0, tiled=True)
    summed = lax.psum(share, "lat")
    whole = lax.all_gather(summed, "lon", axis=0, tiled=True)
    results = []
    offset = 0
    for piece in partial_grads:
        results.append(whole[offset : offset + piece.size].reshape(piece.shape))
        offset = offset + piece.size
    grad_w_one, grad_b_one, grad_w_two, grad_b_two = results
    return (grad_input, grad_w_one, grad_b_one, grad_w_two, grad_b_two)


def solution(mesh):
    placed = (P("lat", "lon", None, None), P("lat", "lon", None, None), P(), P(), P(), P())
    return jax.shard_map(
        on_device,
        mesh=mesh,
        in_specs=placed,
        out_specs=(P("lat", "lon", None, None), P(), P(), P(), P()),
        check_vma=False,
    )
```

profile of v0, /device:TPU:0, one launch (start us, length us, event | category | flops | bytes accessed | tf_op | source)
XLA Modules:
  0.0 626.7 jit_solution(1061869455097390078)
XLA Ops:
  8.1 14.8 %fusion.56 = f32[2,96,96,90]{1,2,3,0:T(8,128)} fusion(f32[1,96,90,180]{1,0,3,2:T(1,128)} %param.7, f32[180,1,96]{2,0,1:T(8,128)S(1)} %get-tuple-element.44, f32[180,1,96]{2,0,1:T(8,128)S(1)} %get-tuple-element.43), kind=kOutput, calls=%fused_computation.52 | convolution fusion | flops 3583215360 | bytes 12994560 | tf_op jit(solution)/shard_map/schw,wqk->qsckh/dot_general | solution.py:106
  23.0 12.4 %copy.98 = f32[2,96,96,90]{3,2,0,1:T(8,128)} copy(f32[2,96,96,90]{1,2,3,0:T(8,128)} %fusion.56) | data formatting | bytes 13271040 | tf_op jit(solution)/shard_map/reshape.2
  36.1 14.5 %fusion.50 = f32[2,1,96,96,90]{3,4,2,0,1:T(8,128)} fusion(f32[2,96,96,90]{3,2,0,1:T(8,128)} %copy.98, f32[1,90,2,90]{1,3,0,2:T(8,128)S(1)} %get-tuple-element.38, f32[1,90,2,90]{1,3,0,2:T(8,128)S(1)} %get-tuple-element.41), kind=kOutput, calls=%fused_computation.49 | convolution fusion | flops 3583213056 | bytes 13400640 | tf_op jit(solution)/shard_map/psckh,phqm->qsckm/dot_general | solution.py:109
  50.6 12.5 %copy.150 = f32[2,1,96,96,90]{2,0,4,3,1:T(2,128)} copy(f32[2,1,96,96,90]{3,4,2,0,1:T(8,128)} %fusion.50) | data formatting | bytes 13271040 | tf_op jit(solution)/shard_map/reshape | solution.py:118
  68.6 14.8 %fusion.59 = f32[2,96,96,90]{1,2,3,0:T(8,128)} fusion(f32[1,96,90,180]{1,0,3,2:T(1,128)} %param.6, f32[180,1,96]{2,0,1:T(8,128)S(1)} %get-tuple-element.48, f32[180,1,96]{2,0,1:T(8,128)S(1)} %get-tuple-element.47), kind=kOutput, calls=%fused_computation.53 | convolution fusion | flops 3583215360 | bytes 12994560 | tf_op jit(solution)/shard_map/schw,wqk->qsckh/dot_general | solution.py:106
  83.4 12.4 %copy.103 = f32[2,96,96,90]{3,2,0,1:T(8,128)} copy(f32[2,96,96,90]{1,2,3,0:T(8,128)} %fusion.59) | data formatting | bytes 13271040 | tf_op jit(solution)/shard_map/reshape.7
  95.9 14.5 %fusion.53 = f32[2,1,96,96,90]{3,4,2,0,1:T(8,128)} fusion(f32[2,96,96,90]{3,2,0,1:T(8,128)} %copy.103, f32[1,90,2,90]{1,3,0,2:T(8,128)S(1)} %get-tuple-element.38, f32[1,90,2,90]{1,3,0,2:T(8,128)S(1)} %get-tuple-element.41), kind=kOutput, calls=%fused_computation.50 | convolution fusion | flops 3583213056 | bytes 13400640 | tf_op jit(solution)/shard_map/psckh,phqm->qsckm/dot_general | solution.py:109
  110.4 12.4 %copy.153 = f32[2,1,96,96,90]{2,0,4,3,1:T(2,128)} copy(f32[2,1,96,96,90]{3,4,2,0,1:T(8,128)} %fusion.53) | data formatting | bytes 13271040 | tf_op jit(solution)/shard_map/reshape | solution.py:117
  122.8 45.2 %all-to-all-done = f32[2,1,96,8640]{2,0,1,3:T(2,128)} async-done(((f32[2,1,96,8640]{2,0,1,3:T(2,128)}), f32[2,1,96,8640]{2,0,1,3:T(2,128)}, u32[]{:S(2)}, u32[]{:S(2)}) %all-to-all-start) | async-done | bytes 6635552 | tf_op jit(solution)/shard_map/all_to_all | solution.py:118
  177.3 13.5 %copy.102 = f32[2,1,96,8,1080]{4,2,0,3,1:T(8,128)} copy(f32[2,1,96,8,1080]{2,0,4,3,1:T(2,128)} %bitcast.29) | data formatting | bytes 13271040 | tf_op jit(solution)/shard_map/all_to_all | solution.py:118
  190.8 81.3 %all-to-all-done.1 = f32[2,1,96,8640]{2,0,1,3:T(2,128)} async-done(((f32[2,1,96,8640]{2,0,1,3:T(2,128)}), f32[2,1,96,8640]{2,0,1,3:T(2,128)}, u32[]{:S(2)}, u32[]{:S(2)}) %all-to-all-start.1) | async-done | bytes 6635552 | tf_op jit(solution)/shard_map/all_to_all | solution.py:117
  272.1 13.5 %copy.107 = f32[2,1,96,8,1080]{4,2,0,3,1:T(8,128)} copy(f32[2,1,96,8,1080]{2,0,4,3,1:T(2,128)} %bitcast.43) | data formatting | bytes 13271040 | tf_op jit(solution)/shard_map/all_to_all | solution.py:117
  285.6 9.7 %fusion.43 = f32[8,2,96,1080,1]{3,2,4,1,0:T(8,128)S(1)} fusion(f32[2,1,96,8,1080]{4,2,0,3,1:T(8,128)} %copy.107, f32[8,1,96,2,96]{2,4,1,3,0:T(8,128)S(1)} %get-tuple-element.36, f32[8,1,96,2,96]{2,4,1,3,0:T(8,128)S(1)} %get-tuple-element.35), kind=kOutput, calls=%fused_computation.44 | convolution fusion | flops 3822354432 | bytes 14450688 | tf_op jit(solution)/shard_map/psbir,bpiqj->qsbjr/dot_general | solution.py:44
  295.4 11.7 %fusion.121 = (f32[2,8,96]{2,0,1:T(2,128)S(1)}, f32[2,1,8,96,1080]{4,3,0,2,1:T(8,128)S(1)}) fusion(f32[2,8,96]{2,0,1:T(2,128)S(1)} %copy.109, f32[2,8,96]{2,0,1:T(2,128)S(1)} %copy.108, f32[8,2,96,1080,1]{3,2,4,1,0:T(8,128)S(1)} %fusion.43, f32[8,1,96,2,96]{2,4,1,3,0:T(8,128)S(1)} %copy-done.5, f32[8,1,96,2,96]{2,4,1,3,0:T(8,128)S(1)} %copy-done.4, ...), kind=kOutput, calls=%fused_computation.153 | convolution fusion | flops 3845577216 | bytes 21104640 | tf_op jit(solution)/shard_map/psbir,bpiqj->qsbjr/dot_general | solution.py:44
  309.9 12.7 %fusion.31 = f32[8,2,96,2,96]{4,2,3,1,0:T(8,128)} fusion(f32[2,1,8,96,1080]{4,3,0,2,1:T(8,128)S(1)} %get-tuple-element.53, f32[8,2,96,1080,1]{3,2,4,1,0:T(8,128)S(1)} %fusion.43, f32[2,8,96]{2,0,1:T(2,128)S(1)} %copy.108), kind=kOutput, calls=%fused_computation.32 | convolution fusion | flops 3836989440 | bytes 14456832 | tf_op jit(solution)/shard_map/psbir,qsbjr->bpiqj/dot_general | solution.py:52
  322.6 15.4 %fusion.122 = (f32[2,8,96]{2,0,1:T(2,128)S(1)}, f32[2,1,8,96,1080]{4,3,0,2,1:T(8,128)S(1)}) fusion(f32[2,8,96]{2,0,1:T(2,128)S(1)} %copy.108, f32[8,2,96,1080,1]{3,2,4,1,0:T(8,128)S(1)} %fusion.43, f32[2,1,8,96,1080]{4,3,0,2,1:T(8,128)} %copy-done.13, f32[8,1,96,2,96]{2,4,1,3,0:T(8,128)} %get-tuple-element.34, f32[8,1,96,2,96]{2,4,1,3,0:T(8,128)S(1)} %copy-done.4), kind=kOutput, calls=%fused_computation.154 | convolution fusion | flops 3855530496 | bytes 21098496 | tf_op jit(solution)/shard_map/qsbjr,bpiqj->psbir/dot_general | solution.py:48
  355.4 56.3 %all-reduce.6.cloned.1.call-done = f32[297984]{0:T(1024)} async-done(((f32[297984]{0:T(1024)}), f32[297984]{0:T(1024)}) %all-reduce.6.cloned.1.call-update) | async-done | bytes 1191952
  413.5 35.1 %all-reduce.4.cloned.1.call-done = f32[37248]{0:T(1024)} async-done(((f32[37248]{0:T(1024)}), f32[37248]{0:T(1024)}) %all-reduce.4.cloned.1.call-update) | async-done | bytes 149008 | tf_op jit(solution)/shard_map/psum | solution.py:133
  450.3 9.9 %fusion.47 = f32[2,1,8,96,1080]{4,3,0,2,1:T(8,128)S(1)} fusion(f32[2,1,8,96,1080]{4,3,0,2,1:T(8,128)} %copy-done, f32[8,1,96,2,96]{2,4,1,3,0:T(8,128)S(1)} %get-tuple-element.36, f32[8,1,96,2,96]{2,4,1,3,0:T(8,128)S(1)} %get-tuple-element.35), kind=kOutput, calls=%fused_computation.48 | convolution fusion | flops 3822354432 | bytes 14450688 | tf_op jit(solution)/shard_map/qsbjr,bpiqj->psbir/dot_general | solution.py:48
  463.6 11.4 %copy.113 = f32[2,1,768,1080]{3,0,1,2:T(2,128)} copy(f32[2,1,768,1080]{3,2,0,1:T(8,128)} %bitcast.261) | data formatting | bytes 13271040 | tf_op jit(solution)/shard_map/reshape | solution.py:82
  486.3 74.0 %all-to-all-done.2 = f32[2,1,768,1080]{3,0,1,2:T(2,128)} async-done(((f32[2,1,768,1080]{3,0,1,2:T(2,128)}), f32[2,1,768,1080]{3,0,1,2:T(2,128)}, u32[]{:S(2)}, u32[]{:S(2)}) %all-to-all-start.2) | async-done | bytes 6635552 | tf_op jit(solution)/shard_map/all_to_all | solution.py:123
  570.8 10.7 %reshape.678 = f32[2,96,96,90,1]{3,2,0,1,4:T(8,128)} reshape(f32[2,1,96,8,1080]{4,3,0,2,1:T(8,128)} %copy.156) | data formatting | bytes 13271040 | tf_op jit(solution)/shard_map/reshape.40
  581.5 13.5 %convolution_bitcast_fusion = f32[2,96,96,90]{2,3,1,0:T(8,128)S(1)} fusion(f32[2,96,96,90,1]{3,2,0,1,4:T(8,128)} %reshape.678, f32[1,90,2,90]{1,3,2,0:T(8,128)S(1)} %copy-done.7, f32[1,90,2,90]{1,3,2,0:T(8,128)S(1)} %copy-done.6), kind=kOutput, calls=%fused_computation.51 | convolution fusion | flops 3583213056 | bytes 13400640 | tf_op jit(solution)/shard_map/psckm,pmqh->qsckh/dot_general | solution.py:127
  594.9 15.3 %fusion.62 = f32[1,96,90,180]{1,3,2,0:T(8,128)S(1)} fusion(f32[2,96,96,90]{2,3,1,0:T(8,128)S(1)} %convolution_bitcast_fusion, f32[1,96,180]{1,2,0:T(8,128)S(1)} %get-tuple-element.46, f32[1,96,180]{1,2,0:T(8,128)S(1)} %get-tuple-element.45), kind=kOutput, calls=%fused_computation.54 | convolution fusion | flops 3583215360 | bytes 12994560 | tf_op jit(solution)/shard_map/qsckh,qkw->schw/dot_general | solution.py:125
  (88 shorter events, 74.1 us)
Async XLA Ops:
  7.2 0.5 copy-start.10
  63.1 104.9 %all-to-all-start = ((f32[2,1,96,8640]{2,0,1,3:T(2,128)}), f32[2,1,96,8640]{2,0,1,3:T(2,128)}, u32[]{:S(2)}, u32[]{:S(2)}) async-start(f32[2,1,96,8640]{2,0,1,3:T(2,128)} %bitcast.260), calls=%async_computation | async-start | bytes 17694720 | tf_op jit(solution)/shard_map/all_to_all | solution.py:118
  168.0 5.7 copy-start.8
  168.0 5.7 copy-start.9
  168.0 5.7 copy-start.3
  168.0 104.1 %all-to-all-start.1 = ((f32[2,1,96,8640]{2,0,1,3:T(2,128)}), f32[2,1,96,8640]{2,0,1,3:T(2,128)}, u32[]{:S(2)}, u32[]{:S(2)}) async-start(f32[2,1,96,8640]{2,0,1,3:T(2,128)} %bitcast.259), calls=%async_computation.1 | async-start | bytes 17694720 | tf_op jit(solution)/shard_map/all_to_all | solution.py:117
  173.1 238.6 %all-reduce.6.cloned.1.call-start = ((), (), s32[]{:S(2)}) async-start(), calls=%async_computation.5 | async-start | bytes 2383872
  285.6 9.8 %copy-start.1 = (f32[2,1,96,8,1080]{4,2,0,3,1:T(8,128)S(1)}, f32[2,1,96,8,1080]{4,2,0,3,1:T(8,128)}, u32[]{:S(2)}) copy-start(f32[2,1,96,8,1080]{4,2,0,3,1:T(8,128)} %copy.102) | copy-start | bytes 19906564
  285.6 9.8 %copy-start.4 = (f32[8,1,96,2,96]{2,4,1,3,0:T(8,128)S(1)}, f32[8,1,96,2,96]{2,4,1,3,0:T(8,128)}, u32[]{:S(2)}) copy-start(f32[8,1,96,2,96]{2,4,1,3,0:T(8,128)} %get-tuple-element.33) | copy-start | bytes 1769476
  285.6 9.8 %copy-start.5 = (f32[8,1,96,2,96]{2,4,1,3,0:T(8,128)S(1)}, f32[8,1,96,2,96]{2,4,1,3,0:T(8,128)}, u32[]{:S(2)}) copy-start(f32[8,1,96,2,96]{2,4,1,3,0:T(8,128)} %get-tuple-element.34) | copy-start | bytes 1769476
  307.1 2.9 copy-start.13
  309.9 28.1 %slice-start = ((s8[7077888]{0:T(1024)(128)(4,1)}), s8[4194304]{0:T(1024)(128)(4,1)S(1)}, s32[]{:S(2)}) async-start(s8[7077888]{0:T(1024)(128)(4,1)} %bitcast.257), calls=%async_computation.6 | async-start | bytes 8388608
  322.6 15.5 %slice-start.1 = ((s8[7077888]{0:T(1024)(128)(4,1)}), s8[2883584]{0:T(1024)(128)(4,1)S(1)}, s32[]{:S(2)}) async-start(s8[7077888]{0:T(1024)(128)(4,1)} %bitcast.257), calls=%async_computation.7 | async-start | bytes 5767168
  338.0 8.7 %copy-start = (f32[2,1,8,96,1080]{4,3,0,2,1:T(8,128)}, f32[2,1,8,96,1080]{4,3,0,2,1:T(8,128)S(1)}, u32[]{:S(2)}) copy-start(f32[2,1,8,96,1080]{4,3,0,2,1:T(8,128)S(1)} %get-tuple-element.55) | copy-start | bytes 19906564
  338.1 9.5 %copy-start.2 = (f32[8,2,96,2,96]{4,2,3,1,0:T(8,128)S(1)}, f32[8,2,96,2,96]{4,2,3,1,0:T(8,128)}, u32[]{:S(2)}) copy-start(f32[8,2,96,2,96]{4,2,3,1,0:T(8,128)} %fusion.31) | copy-start | bytes 3538948
  346.7 7.4 %copy-start.12 = (u32[32]{0:T(128)S(1)}, u32[32]{0:T(128)}, u32[]{:S(2)}) copy-start(u32[32]{0:T(128)} %constant.64) | copy-start | bytes 388
  354.1 94.5 %all-reduce.4.cloned.1.call-start = ((), (), s32[]{:S(2)}) async-start(), calls=%async_computation.3 | async-start | bytes 303104 | tf_op jit(solution)/shard_map/psum | solution.py:133
  413.4 67.3 %all-gather.3.cloned.1.call-start = ((), (), s32[]{:S(2)}) async-start(), calls=%async_computation.4 | async-start | bytes 1340928 | tf_op jit(solution)/shard_map/all_gather | solution.py:134
  475.0 5.2 copy-start.11
  475.0 85.2 %all-to-all-start.2 = ((f32[2,1,768,1080]{3,0,1,2:T(2,128)}), f32[2,1,768,1080]{3,0,1,2:T(2,128)}, u32[]{:S(2)}, u32[]{:S(2)}) async-start(f32[2,1,768,1080]{3,0,1,2:T(2,128)} %copy.113), calls=%async_computation.2 | async-start | bytes 14155776 | tf_op jit(solution)/shard_map/all_to_all | solution.py:123
  570.8 10.7 %copy-start.6 = (f32[1,90,2,90]{1,3,2,0:T(8,128)S(1)}, f32[1,90,2,90]{1,3,2,0:T(8,128)}, u32[]{:S(2)}) copy-start(f32[1,90,2,90]{1,3,2,0:T(8,128)} %get-tuple-element.37) | copy-start | bytes 194404
  570.8 10.7 %copy-start.7 = (f32[1,90,2,90]{1,3,2,0:T(8,128)S(1)}, f32[1,90,2,90]{1,3,2,0:T(8,128)}, u32[]{:S(2)}) copy-start(f32[1,90,2,90]{1,3,2,0:T(8,128)} %get-tuple-element.42) | copy-start | bytes 194404
Sparse Core Ops, SparseCore 0:
  354.2 57.4 all-reduce.5
  414.7 33.8 all-reduce.3
  451.0 24.1 all-gather.2
where the time goes:
time: 637 us; the launch traced here: 627 us
  waiting for transfers between devices  292 us (46%)
  matrix products  156 us (24%)
  local copies, waits for them, and re-layouts  139 us (22%)
  starting transfers between devices  16.4 us (3%)
  between operations  15 us (2%)
  other arithmetic  8.95 us (1%)
    all_to_all x1, waiting for transfers between devices, on_device(): lax.all_to_all(x_both.reshape(flat_shape), 'lon', split_axis=3, concat_ax...  81.3 us
    all_to_all x1, waiting for transfers between devices, on_device(): lax.all_to_all(d_stack, 'lon', split_axis=2, concat_axis=3, tiled=True)  74 us
    unnamed x4, waiting for transfers between devices  56.4 us
    all_to_all x1, waiting for transfers between devices, on_device(): lax.all_to_all(g_both.reshape(flat_shape), 'lon', split_axis=3, concat_ax...  45.2 us
    another operation x4, local copies, waits for them, and re-layouts  42.5 us
    psum x1, waiting for transfers between devices, on_device(): summed = lax.psum(share, 'lat')  35.1 us
    dot_general x2, matrix products, lon_forward(): return jnp.einsum('schw,wqk->qsckh', data, table, precision=HIGHEST)  29.7 us
    dot_general x2, matrix products, lat_forward(): return jnp.einsum('psckh,phqm->qsckm', data, lat_table, precision=HIGHEST)  29.1 us
  transfers between devices with their start and end apart: 6, of which 5 were waited for; matrix products, arithmetic and copies ran while one was open for 16% of the time, Pallas kernels for 0%

commit v1 on v0

--- a/solution.py
+++ b/solution.py
@@ -8,6 +8,22 @@
 GELU_SCALE = math.sqrt(2.0 / math.pi)
 GELU_CUBE = 0.044715
 HIGHEST = lax.Precision.HIGHEST
+
+
+def pairwise_exchange(x, axis, split, join):
+    ways, here = (lax.axis_size(axis), lax.axis_index(axis))
+    width = x.shape[split] // ways
+    dims = list(x.shape)
+    dims[split] = width
+    height = dims[join]
+    dims[join] = height * ways
+    full = jnp.zeros(dims, x.dtype)
+    for mask in range(ways):
+        part = lax.dynamic_slice_in_dim(x, (here ^ mask) * width, width, axis=split)
+        if mask:
+            part = lax.ppermute(part, axis, [(d, d ^ mask) for d in range(ways)])
+        full = lax.dynamic_update_slice_in_dim(full, part, (here ^ mask) * height, axis=join)
+    return full
 
 
 def tables(length, count, limit):
@@ -115,7 +131,7 @@
     flat_shape = (2, samples, local_ch, freq_slots * lat_rows)
     x_modes, g_modes = (
         lax.all_to_all(x_both.reshape(flat_shape), "lon", split_axis=3, concat_axis=2, tiled=True),
-        lax.all_to_all(g_both.reshape(flat_shape), "lon", split_axis=3, concat_axis=2, tiled=True),
+        pairwise_exchange(g_both.reshape(flat_shape), "lon", 3, 2),
     )
     d_stack, partial_grads = block_backward(
         x_modes, g_modes, first_weight, first_bias, second_weight, second_bias

time: 637 us -> 605 us (0.950)
  waiting for transfers between devices: 292 us -> 245 us
  local copies, waits for them, and re-layouts: 139 us -> 153 us
    all_to_all x1, waiting for transfers between devices: 81.3 us -> 0.01 us  [on_device(): lax.all_to_all(x_both.reshape(flat_shape), 'lon', split_axis=3, concat_ax...]
    ppermute x0 -> x7, waiting for transfers between devices: none -> 79 us  [pairwise_exchange(): part = lax.ppermute(part, axis, [(d, d ^ mask) for d in range(ways)])]
    all_to_all x1 -> x0, waiting for transfers between devices: 45.2 us -> none  [on_device(): lax.all_to_all(g_both.reshape(flat_shape), 'lon', split_axis=3, concat_ax...]
    all_to_all x1 -> x0, local copies, waits for them, and re-layouts: 13.5 us -> none  [on_device(): lax.all_to_all(g_both.reshape(flat_shape), 'lon', split_axis=3, concat_ax...]
    dynamic_update_slice x0 -> x7, local copies, waits for them, and re-layouts: none -> 12.9 us  [pairwise_exchange(): lax.dynamic_update_slice_in_dim(full, part, (here ^ mask) * height, axis=...]
    transpose x0 -> x1, local copies, waits for them, and re-layouts: none -> 9.74 us  [lat_forward(): return jnp.einsum('psckh,phqm->qsckm', data, lat_table, precision=HIGHEST)]
    ppermute x0 -> x7, starting transfers between devices: none -> 7.22 us  [pairwise_exchange(): part = lax.ppermute(part, axis, [(d, d ^ mask) for d in range(ways)])]
    unnamed x42 -> x46, local copies, waits for them, and re-layouts: 17.5 us -> 20.7 us
  transfers between devices with their start and end apart: 6 -> 12, of which waited for: 5 -> 7; matrix products, arithmetic and copies ran while one was open for 16% -> 19% of each run, Pallas kernels for 0% -> 0%
where the time goes in v1:
time: 605 us; the launch traced here: 595 us
  waiting for transfers between devices  245 us (40%)
  matrix products  156 us (26%)
  local copies, waits for them, and re-layouts  153 us (25%)
  starting transfers between devices  17.8 us (3%)
  between operations  15.4 us (3%)
  other arithmetic  7.32 us (1%)
    ppermute x7, waiting for transfers between devices, pairwise_exchange(): part = lax.ppermute(part, axis, [(d, d ^ mask) for d in range(ways)])  79 us
    all_to_all x1, waiting for transfers between devices, on_device(): lax.all_to_all(d_stack, 'lon', split_axis=2, concat_axis=3, tiled=True)  74 us
    unnamed x4, waiting for transfers between devices  56.7 us
    another operation x4, local copies, waits for them, and re-layouts  42.5 us
    psum x1, waiting for transfers between devices, on_device(): summed = lax.psum(share, 'lat')  35.1 us
    dot_general x2, matrix products, lon_forward(): return jnp.einsum('schw,wqk->qsckh', data, table, precision=HIGHEST)  29.7 us
    dot_general x2, matrix products, lat_forward(): return jnp.einsum('psckh,phqm->qsckm', data, lat_table, precision=HIGHEST)  29 us
    dot_general x2, matrix products, back_mix(): return jnp.einsum('qsbjr,bpiqj->psbir', left, matrix, precision=HIGHEST)  25.7 us
  transfers between devices with their start and end apart: 12, of which 7 were waited for; matrix products, arithmetic and copies ran while one was open for 19% of the time, Pallas kernels for 0%

profile of v1, /device:TPU:0, one launch (start us, length us, event | category | flops | bytes accessed | tf_op | source)
XLA Modules:
  0.0 594.8 jit_solution(5855833131593109562)
XLA Ops:
  8.1 14.9 %fusion.57 = f32[2,96,96,90]{1,2,3,0:T(8,128)} fusion(f32[1,96,90,180]{1,0,3,2:T(1,128)} %param.6, f32[180,1,96]{2,0,1:T(8,128)S(1)} %get-tuple-element.56, f32[180,1,96]{2,0,1:T(8,128)S(1)} %get-tuple-element.55), kind=kOutput, calls=%fused_computation.53 | convolution fusion | flops 3583215360 | bytes 12994560 | tf_op jit(solution)/shard_map/schw,wqk->qsckh/dot_general | solution.py:122
  23.0 12.4 %copy.98 = f32[2,96,96,90]{3,2,0,1:T(8,128)} copy(f32[2,96,96,90]{1,2,3,0:T(8,128)} %fusion.57) | data formatting | bytes 13271040 | tf_op jit(solution)/shard_map/reshape.6
  36.1 14.5 %fusion.51 = f32[2,1,96,96,90]{3,4,2,0,1:T(8,128)} fusion(f32[2,96,96,90]{3,2,0,1:T(8,128)} %copy.98, f32[1,90,2,90]{1,3,0,2:T(8,128)S(1)} %get-tuple-element.46, f32[1,90,2,90]{1,3,0,2:T(8,128)S(1)} %get-tuple-element.49), kind=kOutput, calls=%fused_computation.50 | convolution fusion | flops 3583213056 | bytes 13400640 | tf_op jit(solution)/shard_map/psckh,phqm->qsckm/dot_general | solution.py:125
  50.6 13.0 %copy.146 = f32[2,1,96,96,90]{2,0,4,3,1:T(2,128)} copy(f32[2,1,96,96,90]{3,4,2,0,1:T(8,128)} %fusion.51) | data formatting | bytes 13271040 | tf_op jit(solution)/shard_map/reshape | solution.py:133
  69.1 14.9 %fusion.54 = f32[2,96,96,90]{1,2,3,0:T(8,128)} fusion(f32[1,96,90,180]{1,0,3,2:T(1,128)} %param.7, f32[180,1,96]{2,0,1:T(8,128)S(1)} %get-tuple-element.52, f32[180,1,96]{2,0,1:T(8,128)S(1)} %get-tuple-element.51), kind=kOutput, calls=%fused_computation.52 | convolution fusion | flops 3583215360 | bytes 12994560 | tf_op jit(solution)/shard_map/schw,wqk->qsckh/dot_general | solution.py:122
  83.9 12.4 %copy.96 = f32[2,96,96,90]{3,2,0,1:T(8,128)} copy(f32[2,96,96,90]{1,2,3,0:T(8,128)} %fusion.54) | data formatting | bytes 13271040 | tf_op jit(solution)/shard_map/reshape.2
  96.3 14.5 %fusion.48 = f32[2,1,96,96,90]{3,4,2,0,1:T(8,128)} fusion(f32[2,96,96,90]{3,2,0,1:T(8,128)} %copy.96, f32[1,90,2,90]{1,3,0,2:T(8,128)S(1)} %get-tuple-element.46, f32[1,90,2,90]{1,3,0,2:T(8,128)S(1)} %get-tuple-element.49), kind=kOutput, calls=%fused_computation.49 | convolution fusion | flops 3583213056 | bytes 13400640 | tf_op jit(solution)/shard_map/psckh,phqm->qsckm/dot_general | solution.py:125
  120.6 10.2 %reshape.640 = f32[2,1,96,8640]{3,2,0,1:T(8,128)} reshape(f32[2,1,96,96,90]{4,3,2,0,1:T(8,128)} %copy.97) | data formatting | bytes 13271040 | tf_op jit(solution)/shard_map/reshape | solution.py:134
  154.5 32.5 %collective-permute-done.1 = f32[2,1,96,1080]{3,2,0,1:T(8,128)} collective-permute-done((f32[2,1,96,1080]{3,2,0,1:T(8,128)}, f32[2,1,96,1080]{3,2,0,1:T(8,128)}, u32[]{:S(2)}, u32[]{:S(2)}) %collective-permute-start.1) | collective-permute-done | bytes 829472 | tf_op jit(solution)/shard_map/ppermute | solution.py:24
  189.3 15.3 %collective-permute-done.2 = f32[2,1,96,1080]{3,2,0,1:T(8,128)} collective-permute-done((f32[2,1,96,1080]{3,2,0,1:T(8,128)}, f32[2,1,96,1080]{3,2,0,1:T(8,128)}, u32[]{:S(2)}, u32[]{:S(2)}) %collective-permute-start.2) | collective-permute-done | bytes 829472 | tf_op jit(solution)/shard_map/ppermute | solution.py:24
  211.0 14.8 %collective-permute-done.5 = f32[2,1,96,1080]{3,2,0,1:T(8,128)S(1)} collective-permute-done((f32[2,1,96,1080]{3,2,0,1:T(8,128)}, f32[2,1,96,1080]{3,2,0,1:T(8,128)S(1)}, u32[]{:S(2)}, u32[]{:S(2)}) %collective-permute-start.5) | collective-permute-done | bytes 829472 | tf_op jit(solution)/shard_map/ppermute | solution.py:24
  226.9 16.3 %collective-permute-done.6 = f32[2,1,96,1080]{3,2,0,1:T(8,128)S(1)} collective-permute-done((f32[2,1,96,1080]{3,2,0,1:T(8,128)}, f32[2,1,96,1080]{3,2,0,1:T(8,128)S(1)}, u32[]{:S(2)}, u32[]{:S(2)}) %collective-permute-start.6) | collective-permute-done | bytes 829472 | tf_op jit(solution)/shard_map/ppermute | solution.py:24
  244.2 13.5 %copy.102 = f32[2,1,96,8,1080]{4,2,0,3,1:T(8,128)} copy(f32[2,1,96,8,1080]{2,0,4,3,1:T(2,128)} %bitcast.41) | data formatting | bytes 13271040 | tf_op jit(solution)/shard_map/all_to_all | solution.py:133
  267.4 13.1 %fusion.121 = (f32[2,8,96]{2,0,1:T(2,128)}, f32[2,1,8,96,1080]{4,3,0,2,1:T(8,128)}) fusion(f32[2,8,96]{2,0,1:T(2,128)S(1)} %copy.104, f32[2,8,96]{2,0,1:T(2,128)S(1)} %copy.103, f32[8,2,96,1080,1]{3,2,4,1,0:T(8,128)S(1)} %fusion.41, f32[8,1,96,2,96]{2,4,1,3,0:T(8,128)S(1)} %copy-done.6, f32[8,1,96,2,96]{2,4,1,3,0:T(8,128)S(1)} %get-tuple-element.41, ...), kind=kOutput, calls=%fused_computation.168 | convolution fusion | flops 3845577216 | bytes 21104640 | tf_op jit(solution)/shard_map/psbir,bpiqj->qsbjr/dot_general | solution.py:60
  280.6 15.6 %fusion.122 = (f32[2,8,96]{2,0,1:T(2,128)}, f32[2,1,8,96,1080]{4,3,0,2,1:T(8,128)S(1)}) fusion(f32[2,8,96]{2,0,1:T(2,128)S(1)} %copy.103, f32[8,2,96,1080,1]{3,2,4,1,0:T(8,128)S(1)} %fusion.41, f32[2,1,8,96,1080]{4,3,0,2,1:T(8,128)} %get-tuple-element.61, f32[8,1,96,2,96]{2,4,1,3,0:T(8,128)} %get-tuple-element.42, ...), kind=kOutput, calls=%fused_computation.169 | convolution fusion | flops 3855530496 | bytes 21098496 | tf_op jit(solution)/shard_map/qsbjr,bpiqj->psbir/dot_general | solution.py:64
  304.9 11.7 %fusion.31 = f32[8,2,96,2,96]{4,2,3,1,0:T(8,128)S(1)} fusion(f32[2,1,8,96,1080]{4,3,0,2,1:T(8,128)S(1)} %copy-done.15, f32[8,2,96,1080,1]{3,2,4,1,0:T(8,128)S(1)} %fusion.41, f32[2,8,96]{2,0,1:T(2,128)S(1)} %copy.103), kind=kOutput, calls=%fused_computation.32 | convolution fusion | flops 3836989440 | bytes 14456832 | tf_op jit(solution)/shard_map/psbir,qsbjr->bpiqj/dot_general | solution.py:68
  322.9 56.7 %all-reduce.6.cloned.1.call-done = f32[297984]{0:T(1024)} async-done(((f32[297984]{0:T(1024)}), f32[297984]{0:T(1024)}) %all-reduce.6.cloned.1.call-update) | async-done | bytes 1191952
  381.3 35.1 %all-reduce.4.cloned.1.call-done = f32[37248]{0:T(1024)} async-done(((f32[37248]{0:T(1024)}), f32[37248]{0:T(1024)}) %all-reduce.4.cloned.1.call-update) | async-done | bytes 149008 | tf_op jit(solution)/shard_map/psum | solution.py:149
  418.1 10.1 %fusion.45 = f32[2,1,8,96,1080]{4,3,0,2,1:T(8,128)S(1)} fusion(f32[2,1,8,96,1080]{4,3,0,2,1:T(8,128)} %copy-done, f32[8,1,96,2,96]{2,4,1,3,0:T(8,128)S(1)} %get-tuple-element.44, f32[8,1,96,2,96]{2,4,1,3,0:T(8,128)S(1)} %get-tuple-element.43), kind=kOutput, calls=%fused_computation.48 | convolution fusion | flops 3822354432 | bytes 14450688 | tf_op jit(solution)/shard_map/qsbjr,bpiqj->psbir/dot_general | solution.py:64
  431.7 11.4 %copy.109 = f32[2,1,768,1080]{3,0,1,2:T(2,128)} copy(f32[2,1,768,1080]{3,2,0,1:T(8,128)} %bitcast.263) | data formatting | bytes 13271040 | tf_op jit(solution)/shard_map/reshape | solution.py:98
  454.3 74.0 %all-to-all-done.1 = f32[2,1,768,1080]{3,0,1,2:T(2,128)} async-done(((f32[2,1,768,1080]{3,0,1,2:T(2,128)}), f32[2,1,768,1080]{3,0,1,2:T(2,128)}, u32[]{:S(2)}, u32[]{:S(2)}) %all-to-all-start.1) | async-done | bytes 6635552 | tf_op jit(solution)/shard_map/all_to_all | solution.py:139
  538.8 10.6 %reshape.680 = f32[2,96,96,90,1]{3,2,0,1,4:T(8,128)} reshape(f32[2,1,96,8,1080]{4,3,0,2,1:T(8,128)} %copy.149) | data formatting | bytes 13271040 | tf_op jit(solution)/shard_map/reshape.39
  549.4 13.3 %convolution_bitcast_fusion = f32[2,96,96,90]{2,3,1,0:T(8,128)S(1)} fusion(f32[2,96,96,90,1]{3,2,0,1,4:T(8,128)} %reshape.680, f32[1,90,2,90]{1,3,2,0:T(8,128)S(1)} %copy-done.8, f32[1,90,2,90]{1,3,2,0:T(8,128)S(1)} %copy-done.7), kind=kOutput, calls=%fused_computation.51 | convolution fusion | flops 3583213056 | bytes 13400640 | tf_op jit(solution)/shard_map/psckm,pmqh->qsckh/dot_general | solution.py:143
  562.7 15.4 %fusion.60 = f32[1,96,90,180]{1,3,2,0:T(8,128)S(1)} fusion(f32[2,96,96,90]{2,3,1,0:T(8,128)S(1)} %convolution_bitcast_fusion, f32[1,96,180]{1,2,0:T(8,128)S(1)} %get-tuple-element.54, f32[1,96,180]{1,2,0:T(8,128)S(1)} %get-tuple-element.53), kind=kOutput, calls=%fused_computation.54 | convolution fusion | flops 3583215360 | bytes 12994560 | tf_op jit(solution)/shard_map/qsckh,qkw->schw/dot_general | solution.py:141
  (113 shorter events, 113.4 us)
Async XLA Ops:
  63.6 180.6 %all-to-all-start = ((f32[2,1,96,8640]{2,0,1,3:T(2,128)}), f32[2,1,96,8640]{2,0,1,3:T(2,128)}, u32[]{:S(2)}, u32[]{:S(2)}) async-start(f32[2,1,96,8640]{2,0,1,3:T(2,128)} %bitcast.262), calls=%async_computation | async-start | bytes 17694720 | tf_op jit(solution)/shard_map/all_to_all | solution.py:133
  68.8 310.7 %all-reduce.6.cloned.1.call-start = ((), (), s32[]{:S(2)}) async-start(), calls=%async_computation.4 | async-start | bytes 2383872
  133.7 12.1 %copy-start.4 = (f32[2,8,96,96]{3,2,1,0:T(8,128)S(1)}, f32[2,8,96,96]{3,2,1,0:T(8,128)}, u32[]{:S(2)}) copy-start(f32[2,8,96,96]{3,2,1,0:T(8,128)} %param.8) | copy-start | bytes 1769476
  133.7 12.1 %copy-start.5 = (f32[2,8,96,96]{3,2,1,0:T(8,128)S(1)}, f32[2,8,96,96]{3,2,1,0:T(8,128)}, u32[]{:S(2)}) copy-start(f32[2,8,96,96]{3,2,1,0:T(8,128)} %param.10) | copy-start | bytes 1769476
  141.1 8.6 %copy-start.9 = (f32[2,8,96]{2,1,0:T(8,128)S(1)}, f32[2,8,96]{2,1,0:T(8,128)}, u32[]{:S(2)}) copy-start(f32[2,8,96]{2,1,0:T(8,128)} %param.9) | copy-start | bytes 18436
  141.1 8.6 %copy-start.10 = (f32[2,8,96]{2,1,0:T(8,128)S(1)}, f32[2,8,96]{2,1,0:T(8,128)}, u32[]{:S(2)}) copy-start(f32[2,8,96]{2,1,0:T(8,128)} %param.11) | copy-start | bytes 18436
  141.1 8.7 %collective-permute-start = (f32[2,1,96,1080]{3,2,0,1:T(8,128)}, f32[2,1,96,1080]{3,2,0,1:T(8,128)}, u32[]{:S(2)}, u32[]{:S(2)}) collective-permute-start(f32[2,1,96,1080]{3,2,0,1:T(8,128)} %get-tuple-element.31), channel_id=1, source_target_pairs={{0,1},{1,0},{2,3},{3,2},{4,5},{5,4},{6,7},{7,6},{8,9},{9,8},{10,11... | collective-permute-start | bytes 2488328 | tf_op jit(solution)/shard_map/ppermute | solution.py:24
  141.6 45.5 %collective-permute-start.1 = (f32[2,1,96,1080]{3,2,0,1:T(8,128)}, f32[2,1,96,1080]{3,2,0,1:T(8,128)}, u32[]{:S(2)}, u32[]{:S(2)}) collective-permute-start(f32[2,1,96,1080]{3,2,0,1:T(8,128)} %get-tuple-element.30), channel_id=1, source_target_pairs={{0,2},{1,3},{2,0},{3,1},{4,6},{5,7},{6,4},{7,5},{8,10},{9,11},{10,... | collective-permute-start | bytes 2488328 | tf_op jit(solution)/shard_map/ppermute | solution.py:24
  143.8 60.7 %collective-permute-start.2 = (f32[2,1,96,1080]{3,2,0,1:T(8,128)}, f32[2,1,96,1080]{3,2,0,1:T(8,128)}, u32[]{:S(2)}, u32[]{:S(2)}) collective-permute-start(f32[2,1,96,1080]{3,2,0,1:T(8,128)} %get-tuple-element.29), channel_id=1, source_target_pairs={{0,3},{1,2},{2,1},{3,0},{4,7},{5,6},{6,5},{7,4},{8,11},{9,10},{10,... | collective-permute-start | bytes 2488328 | tf_op jit(solution)/shard_map/ppermute | solution.py:24
  143.9 62.8 %collective-permute-start.3 = (f32[2,1,96,1080]{3,2,0,1:T(8,128)}, f32[2,1,96,1080]{3,2,0,1:T(8,128)}, u32[]{:S(2)}, u32[]{:S(2)}) collective-permute-start(f32[2,1,96,1080]{3,2,0,1:T(8,128)} %get-tuple-element.28), channel_id=1, source_target_pairs={{0,4},{1,5},{2,6},{3,7},{4,0},{5,1},{6,2},{7,3},{8,12},{9,13},{10,... | collective-permute-start | bytes 2488328 | tf_op jit(solution)/shard_map/ppermute | solution.py:24
  145.7 63.1 %collective-permute-start.4 = (f32[2,1,96,1080]{3,2,0,1:T(8,128)}, f32[2,1,96,1080]{3,2,0,1:T(8,128)}, u32[]{:S(2)}, u32[]{:S(2)}) collective-permute-start(f32[2,1,96,1080]{3,2,0,1:T(8,128)} %get-tuple-element.27), channel_id=1, source_target_pairs={{0,5},{1,4},{2,7},{3,6},{4,1},{5,0},{6,3},{7,2},{8,13},{9,12},{10,... | collective-permute-start | bytes 2488328 | tf_op jit(solution)/shard_map/ppermute | solution.py:24
  149.8 76.1 %collective-permute-start.5 = (f32[2,1,96,1080]{3,2,0,1:T(8,128)}, f32[2,1,96,1080]{3,2,0,1:T(8,128)S(1)}, u32[]{:S(2)}, u32[]{:S(2)}) collective-permute-start(f32[2,1,96,1080]{3,2,0,1:T(8,128)} %get-tuple-element.26), channel_id=1, source_target_pairs={{0,6},{1,7},{2,4},{3,5},{4,2},{5,3},{6,0},{7,1},{8,14},{9,15},{10,... | collective-permute-start | bytes 2488328 | tf_op jit(solution)/shard_map/ppermute | solution.py:24
  187.1 56.1 %collective-permute-start.6 = (f32[2,1,96,1080]{3,2,0,1:T(8,128)}, f32[2,1,96,1080]{3,2,0,1:T(8,128)S(1)}, u32[]{:S(2)}, u32[]{:S(2)}) collective-permute-start(f32[2,1,96,1080]{3,2,0,1:T(8,128)} %get-tuple-element.25), channel_id=1, source_target_pairs={{0,7},{1,6},{2,5},{3,4},{4,3},{5,2},{6,1},{7,0},{8,15},{9,14},{10,... | collective-permute-start | bytes 2488328 | tf_op jit(solution)/shard_map/ppermute | solution.py:24
  257.7 9.8 %copy-start.3 = (f32[2,1,768,1080]{3,2,0,1:T(8,128)S(1)}, f32[2,1,768,1080]{3,2,0,1:T(8,128)}, u32[]{:S(2)}) copy-start(f32[2,1,768,1080]{3,2,0,1:T(8,128)} %constant_dynamic-update-slice_fusion) | copy-start | bytes 19906564
  257.7 9.8 %copy-start.6 = (f32[8,1,96,2,96]{2,4,1,3,0:T(8,128)S(1)}, f32[8,1,96,2,96]{2,4,1,3,0:T(8,128)}, u32[]{:S(2)}) copy-start(f32[8,1,96,2,96]{2,4,1,3,0:T(8,128)} %get-tuple-element.42) | copy-start | bytes 1769476
  267.4 28.7 %slice-start = ((s8[7077888]{0:T(1024)(128)(4,1)}), s8[4194304]{0:T(1024)(128)(4,1)S(1)}, s32[]{:S(2)}) async-start(s8[7077888]{0:T(1024)(128)(4,1)} %bitcast.260), calls=%async_computation.5 | async-start | bytes 8388608
  280.6 15.6 %slice-start.1 = ((s8[7077888]{0:T(1024)(128)(4,1)}), s8[2883584]{0:T(1024)(128)(4,1)S(1)}, s32[]{:S(2)}) async-start(s8[7077888]{0:T(1024)(128)(4,1)} %bitcast.260), calls=%async_computation.6 | async-start | bytes 5767168
  296.2 8.7 %copy-start = (f32[2,1,8,96,1080]{4,3,0,2,1:T(8,128)}, f32[2,1,8,96,1080]{4,3,0,2,1:T(8,128)S(1)}, u32[]{:S(2)}) copy-start(f32[2,1,8,96,1080]{4,3,0,2,1:T(8,128)S(1)} %get-tuple-element.63) | copy-start | bytes 19906564
  296.2 8.8 %copy-start.15 = (f32[2,1,8,96,1080]{4,3,0,2,1:T(8,128)S(1)}, f32[2,1,8,96,1080]{4,3,0,2,1:T(8,128)}, u32[]{:S(2)}) copy-start(f32[2,1,8,96,1080]{4,3,0,2,1:T(8,128)} %get-tuple-element.61) | copy-start | bytes 19906564
  321.6 94.8 %all-reduce.4.cloned.1.call-start = ((), (), s32[]{:S(2)}) async-start(), calls=%async_computation.2 | async-start | bytes 303104 | tf_op jit(solution)/shard_map/psum | solution.py:149
  381.2 67.5 %all-gather.3.cloned.1.call-start = ((), (), s32[]{:S(2)}) async-start(), calls=%async_computation.3 | async-start | bytes 1340928 | tf_op jit(solution)/shard_map/all_gather | solution.py:150
  443.1 85.2 %all-to-all-start.1 = ((f32[2,1,768,1080]{3,0,1,2:T(2,128)}), f32[2,1,768,1080]{3,0,1,2:T(2,128)}, u32[]{:S(2)}, u32[]{:S(2)}) async-start(f32[2,1,768,1080]{3,0,1,2:T(2,128)} %copy.109), calls=%async_computation.1 | async-start | bytes 14155776 | tf_op jit(solution)/shard_map/all_to_all | solution.py:139
  538.8 10.6 %copy-start.7 = (f32[1,90,2,90]{1,3,2,0:T(8,128)S(1)}, f32[1,90,2,90]{1,3,2,0:T(8,128)}, u32[]{:S(2)}) copy-start(f32[1,90,2,90]{1,3,2,0:T(8,128)} %get-tuple-element.45) | copy-start | bytes 194404
  538.8 10.6 %copy-start.8 = (f32[1,90,2,90]{1,3,2,0:T(8,128)S(1)}, f32[1,90,2,90]{1,3,2,0:T(8,128)}, u32[]{:S(2)}) copy-start(f32[1,90,2,90]{1,3,2,0:T(8,128)} %get-tuple-element.50) | copy-start | bytes 194404
  (6 other events, 19.4 us)
Sparse Core Ops, SparseCore 0:
  321.7 57.7 all-reduce.5
  382.5 33.8 all-reduce.3
  418.9 24.1 all-gather.2
